TPU v7x, 128 devices: a whole 4x4x4 slice. The times are simulated.
128 devices in a mesh: wide: 16 (over y, x), narrow: 8 (over z, core).
Axes of the slice: x: 4, y: 4, z: 4, core: 2. Of those that a mesh axis runs over, the one named last changes fastest.
Arguments:
- tokens: bfloat16 [256, 128, 1536], P('wide'), may hold values from -8 to 8
- ln_gain: bfloat16 [1536], replicated, may hold values from 0.3984375 to 1.59375
- gate_weight: bfloat16 [1536, 8960], P(None, 'narrow'), may hold values from -0.15625 to 0.15625
- up_weight: bfloat16 [1536, 8960], P(None, 'narrow'), may hold values from -0.15625 to 0.15625
- down_weight: bfloat16 [8960, 1536], P('narrow'), may hold values from -0.0625 to 0.0625
- out_gain: bfloat16 [1536], replicated, may hold values from 0.25 to 1.75
- shard_ids: int32 [256], P('wide'), may hold values from 0 to 15, as said below
- slab_old: bfloat16 [262144, 1536], P(('wide', 'narrow')), may hold values from -8 to 8
- queries: bfloat16 [16, 64, 1536], P('wide'), may hold values from -12 to 12
- positives: int32 [16, 64], P('wide'), may hold values from 0 to 262399
- owners: int32 [4], replicated, may hold values from 0 to 15
Outputs:
- index_new: bfloat16 [16, 16, 2, 1536], P('wide', 'narrow')
- losses: float32 [4, 64], replicated
Inputs may be any that keep to these rules, and one draw needn't show every extreme that they name: `shard_ids`: among the 16 passages of one index of wide at most 2 have the same shard id; in every draw one shard id is held by exactly 2 passages of every index of wide.
All inputs are finite; a program needn't handle non-finite values.
Results may differ from a plain program's by a relative error of at most 0.0029.
Values may be sent and summed in bfloat16 or wider, within the bound.
No kernel may reach another device: no remote copies, remote signals or barrier semaphores. Data moves between devices by JAX's collectives and lax.ppermute only.
A program may use at most 128 MiB of HBM per device.

v0:
```python
import math
import jax
import jax.numpy as jnp
from jax import lax
from jax.sharding import PartitionSpec as P

EPS = 1e-06


def spread(x, axis, root):
    mine = lax.axis_index(axis) == root
    return lax.psum(jnp.where(mine, x, jnp.zeros_like(x)), axis)


def rms_scale(values):
    return lax.rsqrt(jnp.mean(values * values, axis=-1, keepdims=True) + EPS)


def local(
    tokens,
    ln_gain,
    gate_weight,
    up_weight,
    down_weight,
    out_gain,
    shard_ids,
    slab_old,
    queries,
    positives,
    owners,
):
    passages, seq_len, width = tokens.shape
    narrow_count = lax.axis_size("narrow")
    wide_count = lax.axis_size("wide")
    narrow_rank = lax.axis_index("narrow")
    wide_rank = lax.axis_index("wide")
    piece_width = width // narrow_count
    capacity = 2 * passages // wide_count
    values = tokens.astype(jnp.float32)
    normed = (values * rms_scale(values) * ln_gain.astype(jnp.float32)).astype(jnp.bfloat16)
    normed = normed.reshape(passages * seq_len, width)
    gate = jnp.dot(normed, gate_weight, preferred_element_type=jnp.float32)
    upward = jnp.dot(normed, up_weight, preferred_element_type=jnp.float32)
    hidden = (jax.nn.silu(gate) * upward).astype(jnp.bfloat16)
    partial_value = jnp.dot(hidden, down_weight, preferred_element_type=jnp.float32)
    pooled_part = jnp.mean(partial_value.reshape(passages, seq_len, width), axis=1)
    token_mean = jnp.mean(values, axis=1)
    offset = narrow_rank * piece_width
    pooled = lax.psum(pooled_part, "narrow") + token_mean
    norm_scale = rms_scale(pooled)
    own_piece = lax.dynamic_slice_in_dim(pooled, offset, piece_width, 1)
    gain_piece = lax.dynamic_slice_in_dim(out_gain.astype(jnp.float32), offset, piece_width, 0)
    embedding = (own_piece * norm_scale * gain_piece).astype(jnp.bfloat16)
    positions = jnp.arange(passages, dtype=jnp.int32)
    earlier = positions[:, None] > positions[None, :]
    same = shard_ids[:, None] == shard_ids[None, :]
    rank = jnp.sum((earlier & same).astype(jnp.int32), axis=1)
    slots = shard_ids * capacity + rank
    dispatch = slots[None, :] == jnp.arange(wide_count * capacity, dtype=jnp.int32)[:, None]
    outgoing = jnp.dot(dispatch.astype(jnp.bfloat16), embedding, preferred_element_type=jnp.float32)
    outgoing = outgoing.astype(jnp.bfloat16).reshape(wide_count, capacity, piece_width)
    numbers = wide_rank * passages + positions
    slot_numbers = jnp.sum(jnp.where(dispatch, numbers[None, :] + 1, 0), axis=1) - 1
    slot_numbers = slot_numbers.reshape(wide_count, capacity, 1)
    arrived, arrived_numbers = (
        lax.all_to_all(
            lax.all_to_all(outgoing, "wide", split_axis=0, concat_axis=0, tiled=True),
            "narrow",
            split_axis=0,
            concat_axis=2,
            tiled=True,
        ),
        lax.all_to_all(
            lax.all_to_all(slot_numbers, "wide", split_axis=0, concat_axis=0, tiled=True),
            "narrow",
            split_axis=0,
            concat_axis=2,
            tiled=True,
        ),
    )
    old_total = slab_old.shape[0] * wide_count * narrow_count
    new_rows = arrived.reshape(-1, width)
    new_numbers = arrived_numbers[:, :, 0].reshape(-1)
    valid = (new_numbers >= 0)[None, :]
    new_global = old_total + new_numbers
    device_linear = wide_rank * narrow_count + narrow_rank
    old_global = device_linear * slab_old.shape[0] + jnp.arange(slab_old.shape[0], dtype=jnp.int32)
    scale = 1.0 / math.sqrt(width)
    contract = (((1,), (1,)), ((), ()))
    block_size = queries.shape[1]
    step_count = owners.shape[0]

    def score_rows(block, positive):
        old_scores = (
            lax.dot_general(block, slab_old, contract, preferred_element_type=jnp.float32) * scale
        )
        new_scores = (
            lax.dot_general(block, new_rows, contract, preferred_element_type=jnp.float32) * scale
        )
        masked = jnp.where(valid, new_scores, -jnp.inf)
        local_max = jnp.maximum(jnp.max(old_scores, axis=1), jnp.max(masked, axis=1))
        hit_old = old_global[None, :] == positive[:, None]
        hit_new = valid & (new_global[None, :] == positive[:, None])
        local_positive = jnp.sum(jnp.where(hit_old, old_scores, 0.0), axis=1) + jnp.sum(
            jnp.where(hit_new, new_scores, 0.0), axis=1
        )
        largest = lax.pmax(local_max, ("wide", "narrow"))
        local_total = jnp.sum(jnp.exp(old_scores - largest[:, None]), axis=1)
        local_total = local_total + jnp.sum(
            jnp.where(valid, jnp.exp(new_scores - largest[:, None]), 0.0), axis=1
        )
        total, picked = lax.psum((local_total, local_positive), ("wide", "narrow"))
        return largest + jnp.log(total) - picked

    def step_body(step, losses):
        owner = owners[step]
        block, positive = (spread(queries[0], "wide", owner), spread(positives[0], "wide", owner))
        loss = score_rows(block, positive)
        return lax.dynamic_update_slice_in_dim(losses, loss[None, :], step, 0)

    start_losses = jnp.zeros((step_count, block_size), jnp.float32)
    losses = lax.fori_loop(0, step_count, step_body, start_losses)
    return (arrived[None], losses)


def solution(mesh):
    return jax.shard_map(
        local,
        mesh=mesh,
        in_specs=(
            P("wide", None, None),
            P(),
            P(None, "narrow"),
            P(None, "narrow"),
            P("narrow", None),
            P(),
            P("wide"),
            P(("wide", "narrow"), None),
            P("wide", None, None),
            P("wide", None),
            P(),
        ),
        out_specs=(P("wide", "narrow", None, None), P()),
        check_vma=False,
    )
```

profile of v0, /device:TPU:1, one launch (start us, length us, event | category | flops | bytes accessed | tf_op | source)
XLA Modules:
  0.0 1026.5 jit_solution(8330299875181176620)
XLA Ops:
  7.2 0.8 convert_element_type.27
  8.1 4.9 convert_reduce_fusion
  13.0 1.5 fusion.5
  14.5 2.7 copy-done.2
  17.2 9.7 fusion.16
  26.9 22.3 %bitcast_reduce_fusion = f32[16,1536]{1,0:T(8,128)} fusion(bf16[1120,1536]{1,0:T(8,128)(2,1)} %param.17, bf16[2048,1536]{1,0:T(8,128)(2,1)} %bitcast.51, bf16[1536,1120]{0,1:T(8,128)(2,1)} %param.16, f32[2048,1120]{0,1:T(8,128)} %fusion.16), kind=kOutput, calls=%fused_computation.19 | convolution fusion | flops 14109745152 | bytes 22446080 | tf_op jit(solution)/shard_map/dot_general | solution.py:45
  49.2 1.5 broadcast_multiply_fusion
  50.8 0.2 convert_reduce_fusion.1
  51.1 0.7 sub.50
  51.8 7.6 all-to-all-start.2
  59.4 1.4 dynamic-slice_convert_fusion
  60.8 4.9 all-to-all-done.2
  65.7 7.6 all-to-all-start.3
  73.2 4.6 all-to-all-done.3
  78.1 32.4 %all-reduce.6.cloned.1.call-done = f32[16,1536]{1,0:T(8,128)} async-done(((f32[16,1536]{1,0:T(8,128)}), f32[16,1536]{1,0:T(8,128)}) %all-reduce.6.cloned.1.call-update) | async-done | bytes 98320 | tf_op jit(solution)/shard_map/psum | solution.py:49
  110.5 1.0 multiply_reduce_fusion
  111.5 0.9 convolution_convert_fusion
  112.5 0.6 reshape.84
  113.1 6.6 all-to-all-start
  119.8 6.3 all-to-all-done
  126.2 7.2 all-to-all-start.1
  133.6 4.4 all-to-all-done.1
  138.0 0.7 broadcast_in_dim.99
  138.8 881.1 %while.14 = (s32[]{:T(128)}, f32[4,64]{1,0:T(4,128)}, s32[4]{0:T(128)}, bf16[1,64,1536]{2,1,0:T(8,128)(2,1)}, bf16[2048,1536]{1,0:T(8,128)(2,1)}, /*index=5*/pre...) while((s32[]{:T(128)}, f32[4,64]{1,0:T(4,128)}, ...), condition=%wide.region_19.20_spmd.clone, body=%wide.region_7.19_spmd.clone.sunk | while | flops 404558592 | bytes 10132520 | solution.py:122
  138.9 1.3 dynamic_slice.21
  140.9 0.7 select_bitcast_fusion.2
  141.6 9.3 psum.59
  150.9 69.7 %all-reduce.8.cloned.1.call-done = bf16[64,1536]{1,0:T(8,128)(2,1)} async-done(((bf16[64,1536]{1,0:T(8,128)(2,1)}), bf16[64,1536]{1,0:T(8,128)(2,1)}) %all-reduce.8.cloned.1.call-update) | async-done | bytes 196624 | tf_op jit(solution)/shard_map/while/body/eval_jaxpr/psum | solution.py:12
  220.6 5.8 fusion.36
  226.4 0.2 select_reduce_fusion.7
  226.6 66.3 %pmax.13 = f32[64]{0:T(128)S(1)} all-reduce(f32[64]{0:T(128)S(1)} %max.11), channel_id=1, replica_groups=mesh['wide'=16,'narrow'=8] {'wide','narrow'}, use_global_device_ids=true, to_apply=%region_11.11 | all-reduce | flops 64 | bytes 512 | tf_op jit(solution)/shard_map/while/body/eval_jaxpr/pmax | solution.py:107
  293.0 1.3 exponential_reduce_fusion.2
  294.4 62.5 %all-reduce.2 = (f32[64]{0:T(128)S(1)}, f32[64]{0:T(128)S(1)}) all-reduce(f32[64]{0:T(128)S(1)} %add.187, f32[64]{0:T(128)S(1)} %add.188), channel_id=1, replica_groups=mesh['wide'=16,'narrow'=8] {'wide','narrow'}, use_global_device_ids=true, to_apply=%region_18.18 | all-reduce | flops 128 | bytes 1024 | tf_op jit(solution)/shard_map/while/body/eval_jaxpr/psum | solution.py:112
  356.9 1.3 dynamic_update_slice.9
  358.2 1.3 dynamic_slice.21
  360.2 0.7 select_bitcast_fusion.2
  361.0 10.9 %psum.59 = s32[64]{0:T(128)S(1)} all-reduce(s32[64]{0:T(128)S(1)} %fusion.37), channel_id=1, replica_groups=mesh['wide'=16,'narrow'=8] {'wide'}, use_global_device_ids=true, to_apply=%region_15.15 | all-reduce | flops 64 | bytes 512 | tf_op jit(solution)/shard_map/while/body/eval_jaxpr/psum | solution.py:12
  371.8 69.6 %all-reduce.8.cloned.1.call-done = bf16[64,1536]{1,0:T(8,128)(2,1)} async-done(((bf16[64,1536]{1,0:T(8,128)(2,1)}), bf16[64,1536]{1,0:T(8,128)(2,1)}) %all-reduce.8.cloned.1.call-update) | async-done | bytes 196624 | tf_op jit(solution)/shard_map/while/body/eval_jaxpr/psum | solution.py:12
  441.4 5.8 fusion.36
  447.2 0.2 select_reduce_fusion.7
  447.4 66.4 %pmax.13 = f32[64]{0:T(128)S(1)} all-reduce(f32[64]{0:T(128)S(1)} %max.11), channel_id=1, replica_groups=mesh['wide'=16,'narrow'=8] {'wide','narrow'}, use_global_device_ids=true, to_apply=%region_11.11 | all-reduce | flops 64 | bytes 512 | tf_op jit(solution)/shard_map/while/body/eval_jaxpr/pmax | solution.py:107
  513.8 1.3 exponential_reduce_fusion.2
  515.2 62.5 %all-reduce.2 = (f32[64]{0:T(128)S(1)}, f32[64]{0:T(128)S(1)}) all-reduce(f32[64]{0:T(128)S(1)} %add.187, f32[64]{0:T(128)S(1)} %add.188), channel_id=1, replica_groups=mesh['wide'=16,'narrow'=8] {'wide','narrow'}, use_global_device_ids=true, to_apply=%region_18.18 | all-reduce | flops 128 | bytes 1024 | tf_op jit(solution)/shard_map/while/body/eval_jaxpr/psum | solution.py:112
  577.7 1.3 dynamic_update_slice.9
  579.0 1.3 dynamic_slice.21
  581.0 1.6 select_bitcast_fusion.2
  582.7 0.7 fusion.37
  583.3 9.0 psum.59
  592.3 69.5 %all-reduce.8.cloned.1.call-done = bf16[64,1536]{1,0:T(8,128)(2,1)} async-done(((bf16[64,1536]{1,0:T(8,128)(2,1)}), bf16[64,1536]{1,0:T(8,128)(2,1)}) %all-reduce.8.cloned.1.call-update) | async-done | bytes 196624 | tf_op jit(solution)/shard_map/while/body/eval_jaxpr/psum | solution.py:12
  661.9 5.8 fusion.36
  667.7 0.2 select_reduce_fusion.7
  667.9 66.3 %pmax.13 = f32[64]{0:T(128)S(1)} all-reduce(f32[64]{0:T(128)S(1)} %max.11), channel_id=1, replica_groups=mesh['wide'=16,'narrow'=8] {'wide','narrow'}, use_global_device_ids=true, to_apply=%region_11.11 | all-reduce | flops 64 | bytes 512 | tf_op jit(solution)/shard_map/while/body/eval_jaxpr/pmax | solution.py:107
  734.2 1.3 exponential_reduce_fusion.2
  735.7 62.5 %all-reduce.2 = (f32[64]{0:T(128)S(1)}, f32[64]{0:T(128)S(1)}) all-reduce(f32[64]{0:T(128)S(1)} %add.187, f32[64]{0:T(128)S(1)} %add.188), channel_id=1, replica_groups=mesh['wide'=16,'narrow'=8] {'wide','narrow'}, use_global_device_ids=true, to_apply=%region_18.18 | all-reduce | flops 128 | bytes 1024 | tf_op jit(solution)/shard_map/while/body/eval_jaxpr/psum | solution.py:112
  798.2 1.3 dynamic_update_slice.9
  799.5 1.3 dynamic_slice.21
  801.5 0.7 select_bitcast_fusion.2
  802.2 11.2 %psum.59 = s32[64]{0:T(128)S(1)} all-reduce(s32[64]{0:T(128)S(1)} %fusion.37), channel_id=1, replica_groups=mesh['wide'=16,'narrow'=8] {'wide'}, use_global_device_ids=true, to_apply=%region_15.15 | all-reduce | flops 64 | bytes 512 | tf_op jit(solution)/shard_map/while/body/eval_jaxpr/psum | solution.py:12
  813.4 68.9 %all-reduce.8.cloned.1.call-done = bf16[64,1536]{1,0:T(8,128)(2,1)} async-done(((bf16[64,1536]{1,0:T(8,128)(2,1)}), bf16[64,1536]{1,0:T(8,128)(2,1)}) %all-reduce.8.cloned.1.call-update) | async-done | bytes 196624 | tf_op jit(solution)/shard_map/while/body/eval_jaxpr/psum | solution.py:12
  882.4 5.8 fusion.36
  888.4 66.3 %pmax.13 = f32[64]{0:T(128)S(1)} all-reduce(f32[64]{0:T(128)S(1)} %max.11), channel_id=1, replica_groups=mesh['wide'=16,'narrow'=8] {'wide','narrow'}, use_global_device_ids=true, to_apply=%region_11.11 | all-reduce | flops 64 | bytes 512 | tf_op jit(solution)/shard_map/while/body/eval_jaxpr/pmax | solution.py:107
  954.7 1.3 exponential_reduce_fusion.2
  956.2 62.5 %all-reduce.2 = (f32[64]{0:T(128)S(1)}, f32[64]{0:T(128)S(1)}) all-reduce(f32[64]{0:T(128)S(1)} %add.187, f32[64]{0:T(128)S(1)} %add.188), channel_id=1, replica_groups=mesh['wide'=16,'narrow'=8] {'wide','narrow'}, use_global_device_ids=true, to_apply=%region_18.18 | all-reduce | flops 128 | bytes 1024 | tf_op jit(solution)/shard_map/while/body/eval_jaxpr/psum | solution.py:112
  1018.7 1.3 dynamic_update_slice.9
  (70 shorter events, 1.8 us)
Async XLA Ops:
  7.2 10.1 copy-start
  7.2 103.3 %all-reduce.6.cloned.1.call-start = ((), (), s32[]{:S(2)}) async-start(), calls=%async_computation.4 | async-start | bytes 196608 | tf_op jit(solution)/shard_map/psum | solution.py:49
  7.2 5.8 copy-start.1
  14.5 2.7 copy-start.2
  26.9 23.8 %copy-start.4 = (s32[16]{0:T(128)S(1)}, s32[16]{0:T(128)}, u32[]{:S(2)}) copy-start(s32[16]{0:T(128)} %param.19) | copy-start | bytes 196
  50.9 26.9 %copy-start.5 = (s32[16]{0:T(128)}, s32[16]{0:T(128)S(1)}, u32[]{:S(2)}) copy-start(s32[16]{0:T(128)S(1)} %multiply_add_fusion.1) | copy-start | bytes 196
  51.8 13.9 %all-to-all-start.2 = ((s32[16,2,1]{1,2,0:T(1,128)}), s32[16,2,1]{1,2,0:T(1,128)}, u32[]{:S(2)}, u32[]{:S(2)}) async-start(s32[16,2,1]{1,2,0:T(1,128)} %bitcast.4), calls=%async_computation.2 | async-start | bytes 16384 | tf_op jit(solution)/shard_map/all_to_all | solution.py:74
  65.7 12.2 %all-to-all-start.3 = ((s32[16,2,1]{1,2,0:T(1,128)}), s32[16,2,1]{1,2,0:T(1,128)S(1)}, u32[]{:S(2)}, u32[]{:S(2)}) async-start(s32[16,2,1]{1,2,0:T(1,128)} %all-to-all-done.2), calls=%async_computation.3 | async-start | bytes 16384 | tf_op jit(solution)/shard_map/all_to_all | solution.py:73
  113.1 13.1 %all-to-all-start = ((bf16[16,2,192]{2,1,0:T(2,128)(2,1)}), bf16[16,2,192]{2,1,0:T(2,128)(2,1)}, u32[]{:S(2)}, u32[]{:S(2)}) async-start(bf16[16,2,192]{2,1,0:T(2,128)(2,1)} %reshape.84), calls=%async_computation | async-start | bytes 32768 | tf_op jit(solution)/shard_map/all_to_all | solution.py:67
  126.2 11.9 %all-to-all-start.1 = ((bf16[16,2,192]{2,1,0:T(2,128)(2,1)}), bf16[16,2,192]{2,1,0:T(2,128)(2,1)S(1)}, u32[]{:S(2)}, u32[]{:S(2)}) async-start(bf16[16,2,192]{2,1,0:T(2,128)(2,1)} %all-to-all-done), calls=%async_computation.1 | async-start | bytes 32768 | tf_op jit(solution)/shard_map/all_to_all | solution.py:66
  138.8 81.8 %all-reduce.8.cloned.1.call-start = ((), (), s32[]{:S(2)}) async-start(), calls=%async_computation.5 | async-start | bytes 393216 | tf_op jit(solution)/shard_map/while/body/eval_jaxpr/psum | solution.py:12
  220.6 5.8 copy-start.3
  358.2 83.2 %all-reduce.8.cloned.1.call-start = ((), (), s32[]{:S(2)}) async-start(), calls=%async_computation.5 | async-start | bytes 393216 | tf_op jit(solution)/shard_map/while/body/eval_jaxpr/psum | solution.py:12
  441.4 5.8 copy-start.3
  579.0 82.9 %all-reduce.8.cloned.1.call-start = ((), (), s32[]{:S(2)}) async-start(), calls=%async_computation.5 | async-start | bytes 393216 | tf_op jit(solution)/shard_map/while/body/eval_jaxpr/psum | solution.py:12
  661.9 5.8 copy-start.3
  799.5 82.9 %all-reduce.8.cloned.1.call-start = ((), (), s32[]{:S(2)}) async-start(), calls=%async_computation.5 | async-start | bytes 393216 | tf_op jit(solution)/shard_map/while/body/eval_jaxpr/psum | solution.py:12
  882.4 5.8 copy-start.3
Sparse Core Ops, SparseCore 0:
  50.9 59.5 all-reduce.5
  142.8 77.7 all-reduce.7
  362.2 79.1 all-reduce.7
  582.8 79.0 all-reduce.7
  803.2 79.1 all-reduce.7
where the time goes:
time: 1030 us
  blocking collectives  556 us (54%)
  waiting for transfers between devices  330 us (32%)
  matrix products  56.9 us (6%)
  starting transfers between devices  29 us (3%)
  other arithmetic  22 us (2%)
  local copies, waits for them, and re-layouts  15.6 us (2%)
  between operations  13.8 us (1%)
    psum x4, waiting for transfers between devices, spread(): return lax.psum(jnp.where(mine, x, jnp.zeros_like(x)), axis)  278 us
    pmax x4, blocking collectives, score_rows(): largest = lax.pmax(local_max, ('wide', 'narrow'))  265 us
    psum x4, blocking collectives, score_rows(): total, picked = lax.psum((local_total, local_positive), ('wide', 'narrow'))  250 us
    psum x4, blocking collectives, spread(): return lax.psum(jnp.where(mine, x, jnp.zeros_like(x)), axis)  40.4 us
    psum x1, waiting for transfers between devices, local(): pooled = lax.psum(pooled_part, 'narrow') + token_mean  32.4 us
    dot_general x4, matrix products, score_rows(): lax.dot_general(block, slab_old, contract, preferred_element_type=jnp.flo...  23.3 us
    dot_general x1, matrix products, local(): jnp.dot(hidden, down_weight, preferred_element_type=jnp.float32)  22.3 us
  transfers between devices with their start and end apart: 9, of which 9 were waited for; matrix products, arithmetic and copies ran while one was open for 0% of the time, Pallas kernels for 0%

commit v1 on v0

--- a/solution.py
+++ b/solution.py
@@ -109,7 +109,7 @@
         local_total = local_total + jnp.sum(
             jnp.where(valid, jnp.exp(new_scores - largest[:, None]), 0.0), axis=1
         )
-        total, picked = lax.psum((local_total, local_positive), ("wide", "narrow"))
+        total, picked = lax.psum(lax.psum((local_total, local_positive), "narrow"), "wide")
         return largest + jnp.log(total) - picked
 
     def step_body(step, losses):

time: 1030 us -> 968 us (0.940)
  blocking collectives: 556 us -> 470 us
  waiting for transfers between devices: 330 us -> 350 us
    psum x4 -> x8, blocking collectives: 250 us -> 174 us  [the longest x4 122 us: score_rows(): lax.psum(lax.psum((local_total, local_positive), 'narrow'), 'wide')]
    psum x4, waiting for transfers between devices: 278 us -> 297 us  [spread(): return lax.psum(jnp.where(mine, x, jnp.zeros_like(x)), axis)]
where the time goes in v1:
time: 968 us; the launch traced here: 960 us
  blocking collectives  470 us (49%)
  waiting for transfers between devices  350 us (36%)
  matrix products  56.9 us (6%)
  starting transfers between devices  29 us (3%)
  other arithmetic  22 us (2%)
  local copies, waits for them, and re-layouts  15.6 us (2%)
  between operations  13.8 us (1%)
    psum x4, waiting for transfers between devices, spread(): return lax.psum(jnp.where(mine, x, jnp.zeros_like(x)), axis)  297 us
    pmax x4, blocking collectives, score_rows(): largest = lax.pmax(local_max, ('wide', 'narrow'))  265 us
    psum x4, blocking collectives, score_rows(): lax.psum(lax.psum((local_total, local_positive), 'narrow'), 'wide')  122 us
    psum x4, blocking collectives, score_rows(): lax.psum((local_total, local_positive), 'narrow')  51.5 us
    psum x1, waiting for transfers between devices, local(): pooled = lax.psum(pooled_part, 'narrow') + token_mean  32.4 us
    psum x4, blocking collectives, spread(): return lax.psum(jnp.where(mine, x, jnp.zeros_like(x)), axis)  30.6 us
    dot_general x4, matrix products, score_rows(): lax.dot_general(block, slab_old, contract, preferred_element_type=jnp.flo...  23.3 us
    dot_general x1, matrix products, local(): jnp.dot(hidden, down_weight, preferred_element_type=jnp.float32)  22.3 us
  transfers between devices with their start and end apart: 9, of which 9 were waited for; matrix products, arithmetic and copies ran while one was open for 0% of the time, Pallas kernels for 0%

profile of v1, /device:TPU:1, one launch (start us, length us, event | category | flops | bytes accessed | tf_op | source)
XLA Modules:
  0.0 960.3 jit_solution(8154722622802800495)
XLA Ops:
  7.2 0.8 convert_element_type.27
  8.1 4.9 convert_reduce_fusion
  13.0 1.5 fusion.5
  14.5 2.7 copy-done.2
  17.2 9.7 %fusion.16 = f32[2048,1120]{0,1:T(8,128)} fusion(bf16[2048,1536]{1,0:T(8,128)(2,1)S(1)} %bitcast.50, bf16[1536,1120]{0,1:T(8,128)(2,1)S(1)} %copy-done), kind=kOutput, calls=%fused_computation.49 | convolution fusion | flops 7046430720 | bytes 18907136 | tf_op jit(solution)/shard_map/dot_general | solution.py:42
  26.9 22.3 %bitcast_reduce_fusion = f32[16,1536]{1,0:T(8,128)} fusion(bf16[1120,1536]{1,0:T(8,128)(2,1)} %param.17, bf16[2048,1536]{1,0:T(8,128)(2,1)} %bitcast.51, bf16[1536,1120]{0,1:T(8,128)(2,1)} %param.16, f32[2048,1120]{0,1:T(8,128)} %fusion.16), kind=kOutput, calls=%fused_computation.19 | convolution fusion | flops 14109745152 | bytes 22446080 | tf_op jit(solution)/shard_map/dot_general | solution.py:45
  49.2 1.5 broadcast_multiply_fusion
  51.1 0.7 sub.50
  51.8 7.6 all-to-all-start.2
  59.4 1.4 dynamic-slice_convert_fusion
  60.8 4.9 all-to-all-done.2
  65.7 7.6 all-to-all-start.3
  73.2 4.6 all-to-all-done.3
  78.1 32.4 %all-reduce.9.cloned.1.call-done = f32[16,1536]{1,0:T(8,128)} async-done(((f32[16,1536]{1,0:T(8,128)}), f32[16,1536]{1,0:T(8,128)}) %all-reduce.9.cloned.1.call-update) | async-done | bytes 98320 | tf_op jit(solution)/shard_map/psum | solution.py:49
  110.5 1.0 multiply_reduce_fusion
  111.5 0.9 convolution_convert_fusion
  112.5 0.6 reshape.84
  113.1 6.6 all-to-all-start
  119.8 6.3 all-to-all-done
  126.2 7.2 all-to-all-start.1
  133.6 4.4 all-to-all-done.1
  138.0 0.7 broadcast_in_dim.99
  138.8 814.9 %while.14 = (s32[]{:T(128)}, f32[4,64]{1,0:T(4,128)}, s32[4]{0:T(128)}, bf16[1,64,1536]{2,1,0:T(8,128)(2,1)}, bf16[2048,1536]{1,0:T(8,128)(2,1)}, /*index=5*/pre...) while((s32[]{:T(128)}, f32[4,64]{1,0:T(4,128)}, ...), condition=%wide.region_21.22_spmd.clone, body=%wide.region_7.21_spmd.clone.sunk | while | flops 404558720 | bytes 10133544 | solution.py:122
  138.9 1.3 dynamic_slice.21
  140.9 0.7 select_bitcast_fusion.2
  141.6 9.3 psum.83
  150.9 69.7 %all-reduce.11.cloned.1.call-done = bf16[64,1536]{1,0:T(8,128)(2,1)} async-done(((bf16[64,1536]{1,0:T(8,128)(2,1)}), bf16[64,1536]{1,0:T(8,128)(2,1)}) %all-reduce.11.cloned.1.call-update) | async-done | bytes 196624 | tf_op jit(solution)/shard_map/while/body/eval_jaxpr/psum | solution.py:12
  220.6 5.8 fusion.36
  226.6 66.3 %pmax.13 = f32[64]{0:T(128)S(1)} all-reduce(f32[64]{0:T(128)S(1)} %max.11), channel_id=1, replica_groups=mesh['wide'=16,'narrow'=8] {'wide','narrow'}, use_global_device_ids=true, to_apply=%region_11.11 | all-reduce | flops 64 | bytes 512 | tf_op jit(solution)/shard_map/while/body/eval_jaxpr/pmax | solution.py:107
  293.0 1.3 exponential_reduce_fusion.2
  294.4 12.9 %all-reduce.4 = (f32[64]{0:T(128)S(1)}, f32[64]{0:T(128)S(1)}) all-reduce(f32[64]{0:T(128)S(1)} %add.191, f32[64]{0:T(128)S(1)} %add.192), channel_id=1, replica_groups=mesh['wide'=16,'narrow'=8] {'narrow'}, use_global_device_ids=true, to_apply=%region_19.19 | all-reduce | flops 128 | bytes 1024 | tf_op jit(solution)/shard_map/while/body/eval_jaxpr/psum | solution.py:112
  307.3 30.6 %all-reduce.5 = (f32[64]{0:T(128)S(1)}, f32[64]{0:T(128)S(1)}) all-reduce(f32[64]{0:T(128)S(1)} %get-tuple-element.312, f32[64]{0:T(128)S(1)} %get-tuple-element.313), channel_id=1, replica_groups=mesh['wide'=16,'narrow'=8] {'wide'}, use_global_device_ids=true, to_apply=%region_20.20 | all-reduce | flops 128 | bytes 1024 | tf_op jit(solution)/shard_map/while/body/eval_jaxpr/psum | solution.py:112
  337.9 1.3 dynamic_update_slice.9
  339.2 1.3 dynamic_slice.21
  341.2 0.7 select_bitcast_fusion.2
  341.9 7.1 psum.83
  349.1 76.5 %all-reduce.11.cloned.1.call-done = bf16[64,1536]{1,0:T(8,128)(2,1)} async-done(((bf16[64,1536]{1,0:T(8,128)(2,1)}), bf16[64,1536]{1,0:T(8,128)(2,1)}) %all-reduce.11.cloned.1.call-update) | async-done | bytes 196624 | tf_op jit(solution)/shard_map/while/body/eval_jaxpr/psum | solution.py:12
  425.6 5.8 fusion.36
  431.6 66.3 %pmax.13 = f32[64]{0:T(128)S(1)} all-reduce(f32[64]{0:T(128)S(1)} %max.11), channel_id=1, replica_groups=mesh['wide'=16,'narrow'=8] {'wide','narrow'}, use_global_device_ids=true, to_apply=%region_11.11 | all-reduce | flops 64 | bytes 512 | tf_op jit(solution)/shard_map/while/body/eval_jaxpr/pmax | solution.py:107
  498.0 1.3 exponential_reduce_fusion.2
  499.4 12.9 %all-reduce.4 = (f32[64]{0:T(128)S(1)}, f32[64]{0:T(128)S(1)}) all-reduce(f32[64]{0:T(128)S(1)} %add.191, f32[64]{0:T(128)S(1)} %add.192), channel_id=1, replica_groups=mesh['wide'=16,'narrow'=8] {'narrow'}, use_global_device_ids=true, to_apply=%region_19.19 | all-reduce | flops 128 | bytes 1024 | tf_op jit(solution)/shard_map/while/body/eval_jaxpr/psum | solution.py:112
  512.3 30.6 %all-reduce.5 = (f32[64]{0:T(128)S(1)}, f32[64]{0:T(128)S(1)}) all-reduce(f32[64]{0:T(128)S(1)} %get-tuple-element.312, f32[64]{0:T(128)S(1)} %get-tuple-element.313), channel_id=1, replica_groups=mesh['wide'=16,'narrow'=8] {'wide'}, use_global_device_ids=true, to_apply=%region_20.20 | all-reduce | flops 128 | bytes 1024 | tf_op jit(solution)/shard_map/while/body/eval_jaxpr/psum | solution.py:112
  542.9 1.3 dynamic_update_slice.9
  544.2 1.3 dynamic_slice.21
  546.2 1.6 select_bitcast_fusion.2
  547.9 0.7 fusion.37
  548.5 5.5 psum.83
  554.1 76.4 %all-reduce.11.cloned.1.call-done = bf16[64,1536]{1,0:T(8,128)(2,1)} async-done(((bf16[64,1536]{1,0:T(8,128)(2,1)}), bf16[64,1536]{1,0:T(8,128)(2,1)}) %all-reduce.11.cloned.1.call-update) | async-done | bytes 196624 | tf_op jit(solution)/shard_map/while/body/eval_jaxpr/psum | solution.py:12
  630.4 5.8 fusion.36
  636.5 66.3 %pmax.13 = f32[64]{0:T(128)S(1)} all-reduce(f32[64]{0:T(128)S(1)} %max.11), channel_id=1, replica_groups=mesh['wide'=16,'narrow'=8] {'wide','narrow'}, use_global_device_ids=true, to_apply=%region_11.11 | all-reduce | flops 64 | bytes 512 | tf_op jit(solution)/shard_map/while/body/eval_jaxpr/pmax | solution.py:107
  702.8 1.3 exponential_reduce_fusion.2
  704.3 12.9 %all-reduce.4 = (f32[64]{0:T(128)S(1)}, f32[64]{0:T(128)S(1)}) all-reduce(f32[64]{0:T(128)S(1)} %add.191, f32[64]{0:T(128)S(1)} %add.192), channel_id=1, replica_groups=mesh['wide'=16,'narrow'=8] {'narrow'}, use_global_device_ids=true, to_apply=%region_19.19 | all-reduce | flops 128 | bytes 1024 | tf_op jit(solution)/shard_map/while/body/eval_jaxpr/psum | solution.py:112
  717.1 30.6 %all-reduce.5 = (f32[64]{0:T(128)S(1)}, f32[64]{0:T(128)S(1)}) all-reduce(f32[64]{0:T(128)S(1)} %get-tuple-element.312, f32[64]{0:T(128)S(1)} %get-tuple-element.313), channel_id=1, replica_groups=mesh['wide'=16,'narrow'=8] {'wide'}, use_global_device_ids=true, to_apply=%region_20.20 | all-reduce | flops 128 | bytes 1024 | tf_op jit(solution)/shard_map/while/body/eval_jaxpr/psum | solution.py:112
  747.7 1.3 dynamic_update_slice.9
  749.0 1.3 dynamic_slice.21
  751.0 0.7 select_bitcast_fusion.2
  751.8 8.7 psum.83
  760.5 74.7 %all-reduce.11.cloned.1.call-done = bf16[64,1536]{1,0:T(8,128)(2,1)} async-done(((bf16[64,1536]{1,0:T(8,128)(2,1)}), bf16[64,1536]{1,0:T(8,128)(2,1)}) %all-reduce.11.cloned.1.call-update) | async-done | bytes 196624 | tf_op jit(solution)/shard_map/while/body/eval_jaxpr/psum | solution.py:12
  835.1 5.8 fusion.36
  841.1 66.3 %pmax.13 = f32[64]{0:T(128)S(1)} all-reduce(f32[64]{0:T(128)S(1)} %max.11), channel_id=1, replica_groups=mesh['wide'=16,'narrow'=8] {'wide','narrow'}, use_global_device_ids=true, to_apply=%region_11.11 | all-reduce | flops 64 | bytes 512 | tf_op jit(solution)/shard_map/while/body/eval_jaxpr/pmax | solution.py:107
  907.5 1.3 exponential_reduce_fusion.2
  908.9 12.9 %all-reduce.4 = (f32[64]{0:T(128)S(1)}, f32[64]{0:T(128)S(1)}) all-reduce(f32[64]{0:T(128)S(1)} %add.191, f32[64]{0:T(128)S(1)} %add.192), channel_id=1, replica_groups=mesh['wide'=16,'narrow'=8] {'narrow'}, use_global_device_ids=true, to_apply=%region_19.19 | all-reduce | flops 128 | bytes 1024 | tf_op jit(solution)/shard_map/while/body/eval_jaxpr/psum | solution.py:112
  921.8 30.6 %all-reduce.5 = (f32[64]{0:T(128)S(1)}, f32[64]{0:T(128)S(1)}) all-reduce(f32[64]{0:T(128)S(1)} %get-tuple-element.312, f32[64]{0:T(128)S(1)} %get-tuple-element.313), channel_id=1, replica_groups=mesh['wide'=16,'narrow'=8] {'wide'}, use_global_device_ids=true, to_apply=%region_20.20 | all-reduce | flops 128 | bytes 1024 | tf_op jit(solution)/shard_map/while/body/eval_jaxpr/psum | solution.py:112
  952.4 1.3 dynamic_update_slice.9
  (74 shorter events, 2.5 us)
Async XLA Ops:
  7.2 10.1 %copy-start = (bf16[1536,1120]{0,1:T(8,128)(2,1)S(1)}, bf16[1536,1120]{0,1:T(8,128)(2,1)}, u32[]{:S(2)}) copy-start(bf16[1536,1120]{0,1:T(8,128)(2,1)} %param.15) | copy-start | bytes 10321924
  7.2 103.3 %all-reduce.9.cloned.1.call-start = ((), (), s32[]{:S(2)}) async-start(), calls=%async_computation.4 | async-start | bytes 196608 | tf_op jit(solution)/shard_map/psum | solution.py:49
  7.2 5.8 copy-start.1
  14.5 2.7 copy-start.2
  26.9 23.8 %copy-start.4 = (s32[16]{0:T(128)S(1)}, s32[16]{0:T(128)}, u32[]{:S(2)}) copy-start(s32[16]{0:T(128)} %param.19) | copy-start | bytes 196
  50.9 26.9 %copy-start.5 = (s32[16]{0:T(128)}, s32[16]{0:T(128)S(1)}, u32[]{:S(2)}) copy-start(s32[16]{0:T(128)S(1)} %multiply_add_fusion.1) | copy-start | bytes 196
  51.8 13.9 %all-to-all-start.2 = ((s32[16,2,1]{1,2,0:T(1,128)}), s32[16,2,1]{1,2,0:T(1,128)}, u32[]{:S(2)}, u32[]{:S(2)}) async-start(s32[16,2,1]{1,2,0:T(1,128)} %bitcast.4), calls=%async_computation.2 | async-start | bytes 16384 | tf_op jit(solution)/shard_map/all_to_all | solution.py:74
  65.7 12.2 %all-to-all-start.3 = ((s32[16,2,1]{1,2,0:T(1,128)}), s32[16,2,1]{1,2,0:T(1,128)S(1)}, u32[]{:S(2)}, u32[]{:S(2)}) async-start(s32[16,2,1]{1,2,0:T(1,128)} %all-to-all-done.2), calls=%async_computation.3 | async-start | bytes 16384 | tf_op jit(solution)/shard_map/all_to_all | solution.py:73
  113.1 13.1 %all-to-all-start = ((bf16[16,2,192]{2,1,0:T(2,128)(2,1)}), bf16[16,2,192]{2,1,0:T(2,128)(2,1)}, u32[]{:S(2)}, u32[]{:S(2)}) async-start(bf16[16,2,192]{2,1,0:T(2,128)(2,1)} %reshape.84), calls=%async_computation | async-start | bytes 32768 | tf_op jit(solution)/shard_map/all_to_all | solution.py:67
  126.2 11.9 %all-to-all-start.1 = ((bf16[16,2,192]{2,1,0:T(2,128)(2,1)}), bf16[16,2,192]{2,1,0:T(2,128)(2,1)S(1)}, u32[]{:S(2)}, u32[]{:S(2)}) async-start(bf16[16,2,192]{2,1,0:T(2,128)(2,1)} %all-to-all-done), calls=%async_computation.1 | async-start | bytes 32768 | tf_op jit(solution)/shard_map/all_to_all | solution.py:66
  138.8 81.8 %all-reduce.11.cloned.1.call-start = ((), (), s32[]{:S(2)}) async-start(), calls=%async_computation.5 | async-start | bytes 393216 | tf_op jit(solution)/shard_map/while/body/eval_jaxpr/psum | solution.py:12
  220.6 5.8 copy-start.3
  339.2 86.4 %all-reduce.11.cloned.1.call-start = ((), (), s32[]{:S(2)}) async-start(), calls=%async_computation.5 | async-start | bytes 393216 | tf_op jit(solution)/shard_map/while/body/eval_jaxpr/psum | solution.py:12
  425.6 5.8 copy-start.3
  544.2 86.2 %all-reduce.11.cloned.1.call-start = ((), (), s32[]{:S(2)}) async-start(), calls=%async_computation.5 | async-start | bytes 393216 | tf_op jit(solution)/shard_map/while/body/eval_jaxpr/psum | solution.py:12
  630.4 5.8 copy-start.3
  749.0 86.1 %all-reduce.11.cloned.1.call-start = ((), (), s32[]{:S(2)}) async-start(), calls=%async_computation.5 | async-start | bytes 393216 | tf_op jit(solution)/shard_map/while/body/eval_jaxpr/psum | solution.py:12
  835.1 5.8 copy-start.3
Sparse Core Ops, SparseCore 0:
  50.9 59.5 all-reduce.8
  142.8 77.7 all-reduce.10
  343.2 82.3 all-reduce.10
  548.0 82.4 all-reduce.10
  752.7 82.3 all-reduce.10
